TPU v7x, 256 devices: a whole 4x4x8 slice. The times are simulated.
256 devices in a mesh: patch: 16 (over z_hi, x), wrow: 4 (over z_lo, core), wcol: 4 (over y).
Axes of the slice: x: 4, y: 4, z: 8 (z_hi: 4, z_lo: 2; z = z_hi * 2 + z_lo), core: 2. Of those that a mesh axis runs over, the one named last changes fastest.
Arguments:
- hidden_states: bfloat16 [4, 8192, 1536], P('wrow', ('patch', 'wcol')), may hold values from -6 to 6
- modulation: float32 [4, 3, 1536], P('wrow'), may hold values from -4 to 4
- w_qkv: bfloat16 [1536, 3, 1536], P('wrow', None, 'wcol'), may hold values from -1 to 1
- w_out: bfloat16 [1536, 1536], P('wcol', 'wrow'), may hold values from -0.15625 to 0.15625
- lengths: int32 [4], P('wrow'), may hold values from 1 to 8192, 20480 in all
Outputs:
- updated: bfloat16 [4, 8192, 1536], P('wrow', ('patch', 'wcol'))
Inputs may be any that keep to these rules, and one draw needn't show every extreme that they name: lengths[v] real tokens in video v, padding after them; the longest video fills all 8192 slots.
All inputs are finite; a program needn't handle non-finite values. No bound on the sum of `lengths` on one device may be relied on, other than what follows from the above.
Results may differ from a plain program's by a relative error of at most 0.015.
The roundings to bfloat16 on the way count: a program that leaves them out, or rounds other values in their place, can miss the bound.
Values may be sent and summed in bfloat16 or wider, within the bound.
A program may use at most 64 MiB of HBM per device.

v0:
```python
import jax
import jax.numpy as jnp
from jax import lax
from jax.sharding import PartitionSpec as P

HD = 128
EPSILON = 1e-06
FLOOR = -1e30


def modulated_norm(states, shift, scale):
    values = states.astype(jnp.float32)
    center = jnp.mean(values, axis=-1, keepdims=True)
    spread = jnp.mean(jnp.square(values - center), axis=-1, keepdims=True)
    return ((values - center) * lax.rsqrt(spread + EPSILON) * (1.0 + scale) + shift).astype(
        jnp.bfloat16
    )


def absorb(carry, keys, values, first, queries, limits):
    peak, weight_sum, numer = carry
    videos_here = keys.shape[0]
    count = keys.shape[1]
    heads_here = queries.shape[2]
    head_size = queries.shape[3]
    key_heads = keys.reshape(videos_here, count, heads_here, head_size)
    value_heads = values.reshape(videos_here, count, heads_here, head_size)
    scores = jnp.einsum(
        "vqhd,vkhd->vhqk", queries, key_heads, preferred_element_type=jnp.float32
    ) * head_size ** (-0.5)
    position = first + jnp.arange(count, dtype=jnp.int32)
    valid = (position[None, :] < limits[:, None])[:, None, None, :]
    scores = jnp.where(valid, scores, FLOOR)
    new_peak = jnp.maximum(peak, jnp.max(scores, axis=-1))
    factor = jnp.exp(peak - new_peak)
    probs = jnp.exp(scores - new_peak[..., None]) * valid.astype(jnp.float32)
    weight_sum = weight_sum * factor + jnp.sum(probs, axis=-1)
    numer = numer * factor[..., None] + jnp.einsum(
        "vhqk,vkhd->vhqd",
        probs.astype(jnp.bfloat16),
        value_heads,
        preferred_element_type=jnp.float32,
    )
    return (new_peak, weight_sum, numer)


def body(hidden_states, modulation, w_qkv, w_out, lengths):
    videos_here = hidden_states.shape[0]
    width = hidden_states.shape[2]
    shift = modulation[:, 0][:, None, :]
    scale = modulation[:, 1][:, None, :]
    gate = modulation[:, 2][:, None, :]
    normed = modulated_norm(hidden_states, shift, scale)
    tile_rows = lax.all_gather(normed, "wcol", axis=1, tiled=True)
    tile_len = tile_rows.shape[1]
    local_cols = w_qkv.shape[2]
    flat_rows = tile_rows.reshape(videos_here * tile_len, width)
    piece = lax.all_gather(w_qkv, "wrow", axis=0, tiled=True)
    mixed = jnp.dot(
        flat_rows, piece.reshape(piece.shape[0], 3 * local_cols), preferred_element_type=jnp.float32
    )
    mixed = mixed.reshape(videos_here, tile_len, 3 * local_cols)
    mixed = mixed.astype(jnp.bfloat16).reshape(videos_here, tile_len, 3, local_cols)
    heads_here = local_cols // HD
    queries = mixed[:, :, 0].reshape(videos_here, tile_len, heads_here, HD)
    keys = mixed[:, :, 1]
    values = mixed[:, :, 2]
    start_peak = jnp.full((videos_here, heads_here, tile_len), FLOOR, jnp.float32)
    start_sum = jnp.zeros((videos_here, heads_here, tile_len), jnp.float32)
    start_numer = jnp.zeros((videos_here, heads_here, tile_len, HD), jnp.float32)
    key_piece = lax.all_gather(keys, "patch", axis=1, tiled=True)
    value_piece = lax.all_gather(values, "patch", axis=1, tiled=True)
    count = key_piece.shape[1]
    block_len = 512

    def one_block(index, inner):
        offset = index * block_len
        key_block = lax.dynamic_slice_in_dim(key_piece, offset, block_len, 1)
        value_block = lax.dynamic_slice_in_dim(value_piece, offset, block_len, 1)
        return absorb(inner, key_block, value_block, offset, queries, lengths)

    peak, weight_sum, numer = lax.fori_loop(
        0, count // block_len, one_block, (start_peak, start_sum, start_numer)
    )
    attended = (numer / weight_sum[..., None]).astype(jnp.bfloat16)
    attended = jnp.transpose(attended, (0, 2, 1, 3)).reshape(videos_here * tile_len, local_cols)
    partial_out = jnp.dot(
        attended,
        lax.all_gather(w_out, "wrow", axis=1, tiled=True),
        preferred_element_type=jnp.float32,
    )
    partial_out = partial_out.reshape(videos_here, tile_len, width)
    out_proj = lax.psum_scatter(
        partial_out.astype(jnp.bfloat16), "wcol", scatter_dimension=1, tiled=True
    ).astype(jnp.float32)
    return (hidden_states.astype(jnp.float32) + gate * out_proj).astype(jnp.bfloat16)


def solution(mesh):
    placed = (
        P("wrow", ("patch", "wcol"), None),
        P("wrow", None, None),
        P("wrow", None, "wcol"),
        P("wcol", "wrow"),
        P("wrow"),
    )
    return jax.shard_map(
        body,
        mesh=mesh,
        in_specs=placed,
        out_specs=P("wrow", ("patch", "wcol"), None),
        check_vma=False,
    )
```

profile of v0, /device:TPU:2, one launch (start us, length us, event | category | flops | bytes accessed | tf_op | source)
XLA Modules:
  0.0 490.6 jit_solution(7066353537932086624)
XLA Ops:
  14.8 29.8 %all-gather.8.cloned.1.call-done = bf16[1,512,1536]{2,1,0:T(8,128)(2,1)} async-done(((bf16[1,128,1536]{2,1,0:T(8,128)(2,1)}), bf16[1,512,1536]{2,1,0:T(8,128)(2,1)}) %all-gather.8.cloned.1.call-update) | async-done | bytes 1572880 | tf_op jit(solution)/shard_map/all_gather | solution.py:54
  44.6 45.2 %all-gather.10.cloned.1.call-done = bf16[1536,3,384]{0,2,1:T(8,128)(2,1)} async-done(((bf16[384,3,384]{0,2,1:T(8,128)(2,1)}), bf16[1536,3,384]{0,2,1:T(8,128)(2,1)}) %all-gather.10.cloned.1.call-update) | async-done | bytes 3538960 | tf_op jit(solution)/shard_map/all_gather | solution.py:58
  89.8 4.7 convolution_convert_fusion
  97.7 103.0 %all-gather.14.cloned.1.call-done = bf16[1,8192,1,384]{1,3,2,0:T(8,128)(2,1)} async-done(((bf16[1,512,1,384]{1,3,2,0:T(8,128)(2,1)}), bf16[1,8192,1,384]{1,3,2,0:T(8,128)(2,1)}) %all-gather.14.cloned.1.call-update) | async-done | bytes 6291472 | tf_op jit(solution)/shard_map/all_gather | solution.py:71
  200.7 104.5 %all-gather.16.cloned.1.call-done = bf16[1,8192,1,384]{1,3,2,0:T(8,128)(2,1)} async-done(((bf16[1,512,1,384]{1,3,2,0:T(8,128)(2,1)}), bf16[1,8192,1,384]{1,3,2,0:T(8,128)(2,1)}) %all-gather.16.cloned.1.call-update) | async-done | bytes 6291472 | tf_op jit(solution)/shard_map/all_gather | solution.py:72
  305.2 143.9 %while.18 = (s32[]{:T(128)}, f32[1,3,512]{2,1,0:T(4,128)S(1)}, f32[1,3,512]{2,1,0:T(4,128)}, f32[1,3,512,128]{3,2,1,0:T(8,128)}, s32[1]{0:T(128)}, /*index=5*/bf...) while((s32[]{:T(128)}, f32[1,3,512]{2,1,0:T(4,128)S(1)}, ...), condition=%wide.region_5.6_spmd.clone, body=%wide.region_2.5_spmd.clone.sunk | while | flops 413477376 | bytes 13930823 | solution.py:82
  309.3 3.2 fusion.46
  318.0 3.5 fusion.46
  327.1 3.4 fusion.46
  336.1 3.4 fusion.46
  345.1 3.4 fusion.46
  354.1 3.4 fusion.46
  363.1 3.4 fusion.46
  372.1 3.4 fusion.46
  381.1 3.4 fusion.46
  390.1 3.4 fusion.46
  399.2 3.4 fusion.46
  408.2 3.4 fusion.46
  417.2 3.4 fusion.46
  426.2 3.4 fusion.46
  435.2 3.4 fusion.46
  444.2 3.4 fusion.46
  451.5 3.4 fusion.17
  454.9 27.0 %reduce-scatter.2.cloned.1.call-done = bf16[1,128,1536]{2,1,0:T(8,128)(2,1)} async-done(((bf16[1,512,1536]{2,1,0:T(8,128)(2,1)}), bf16[1,128,1536]{2,1,0:T(8,128)(2,1)}) %reduce-scatter.2.cloned.1.call-update) | async-done | bytes 393232 | tf_op jit(solution)/shard_map/reduce_scatter | solution.py:93
  (305 shorter events, 103.1 us)
Async XLA Ops:
  6.5 38.1 %all-gather.8.cloned.1.call-start = ((), (), s32[]{:S(2)}) async-start(), calls=%async_computation.1 | async-start | bytes 1966080 | tf_op jit(solution)/shard_map/all_gather | solution.py:54
  12.4 77.4 %all-gather.10.cloned.1.call-start = ((), (), s32[]{:S(2)}) async-start(), calls=%async_computation.2 | async-start | bytes 4423680 | tf_op jit(solution)/shard_map/all_gather | solution.py:58
  14.7 186.0 %all-gather.14.cloned.1.call-start = ((), (), s32[]{:S(2)}) async-start(), calls=%async_computation.5 | async-start | bytes 6684672 | tf_op jit(solution)/shard_map/all_gather | solution.py:71
  96.2 209.0 %all-gather.16.cloned.1.call-start = ((), (), s32[]{:S(2)}) async-start(), calls=%async_computation.6 | async-start | bytes 6684672 | tf_op jit(solution)/shard_map/all_gather | solution.py:72
  96.8 354.7 %all-gather.12.cloned.1.call-start = ((), (), s32[]{:S(2)}) async-start(), calls=%async_computation.3 | async-start | bytes 1474560 | tf_op jit(solution)/shard_map/all_gather | solution.py:89
  97.4 384.6 %reduce-scatter.2.cloned.1.call-start = ((), (), s32[]{:S(2)}) async-start(), calls=%async_computation.4 | async-start | bytes 1966080 | tf_op jit(solution)/shard_map/reduce_scatter | solution.py:93
  318.0 3.5 copy-start.3
  318.0 3.5 copy-start.5
  327.0 3.5 copy-start.3
  336.1 3.5 copy-start.3
  345.1 3.5 copy-start.3
  354.1 3.5 copy-start.3
  363.1 3.5 copy-start.3
  372.1 3.5 copy-start.3
  381.1 3.5 copy-start.3
  390.1 3.5 copy-start.3
  399.1 3.5 copy-start.3
  408.1 3.5 copy-start.3
  417.2 3.5 copy-start.3
  426.2 3.5 copy-start.3
  435.2 3.5 copy-start.3
  444.2 3.5 copy-start.3
  450.6 31.3 %copy-start = (bf16[1,128,1536]{2,1,0:T(8,128)(2,1)S(1)}, bf16[1,128,1536]{2,1,0:T(8,128)(2,1)}, u32[]{:S(2)}) copy-start(bf16[1,128,1536]{2,1,0:T(8,128)(2,1)} %param.7) | copy-start | bytes 1179652
  450.6 31.3 %copy-start.6 = (f32[1536]{0:T(1024)S(1)}, f32[1536]{0:T(1024)}, u32[]{:S(2)}) copy-start(f32[1536]{0:T(1024)} %get-tuple-element.182) | copy-start | bytes 18436
  (64 other events, 91.9 us)
Sparse Core Ops, SparseCore 0:
  12.5 32.0 all-gather.7
  46.4 43.3 all-gather.9
  96.3 104.3 all-gather.13
  203.0 102.2 all-gather.15
  306.9 22.7 all-gather.11
  455.0 26.8 reduce-scatter.1
where the time goes:
time: 492 us; the launch traced here: 491 us
  waiting for transfers between devices  311 us (63%)
  matrix products  76 us (15%)
  local copies, waits for them, and re-layouts  45.7 us (9%)
  other arithmetic  43.1 us (9%)
  between operations  13.6 us (3%)
    all_gather x1, waiting for transfers between devices, body(): value_piece = lax.all_gather(values, 'patch', axis=1, tiled=True)  105 us
    all_gather x1, waiting for transfers between devices, body(): key_piece = lax.all_gather(keys, 'patch', axis=1, tiled=True)  103 us
    dot_general x16, matrix products, absorb(): jnp.einsum('vhqk,vkhd->vhqd', probs.astype(jnp.bfloat16), value_heads, pr...  54.9 us
    all_gather x1, waiting for transfers between devices, body(): piece = lax.all_gather(w_qkv, 'wrow', axis=0, tiled=True)  45.2 us
    dynamic_slice x16, local copies, waits for them, and re-layouts, one_block(): value_block = lax.dynamic_slice_in_dim(value_piece, offset, block_len, 1)  30.6 us
    all_gather x1, waiting for transfers between devices, body(): tile_rows = lax.all_gather(normed, 'wcol', axis=1, tiled=True)  29.8 us
    reduce_scatter x1, waiting for transfers between devices, body(): lax.psum_scatter(partial_out.astype(jnp.bfloat16), 'wcol', scatter_dimens...  27 us
    convert_element_type x16, other arithmetic, absorb(): probs = jnp.exp(scores - new_peak[..., None]) * valid.astype(jnp.float32)  19.9 us
  transfers between devices with their start and end apart: 6, of which 5 were waited for; matrix products, arithmetic and copies ran while one was open for 28% of the time, Pallas kernels for 0%

commit v1 on v0

--- a/solution.py
+++ b/solution.py
@@ -68,7 +68,9 @@
     start_peak = jnp.full((videos_here, heads_here, tile_len), FLOOR, jnp.float32)
     start_sum = jnp.zeros((videos_here, heads_here, tile_len), jnp.float32)
     start_numer = jnp.zeros((videos_here, heads_here, tile_len, HD), jnp.float32)
-    key_piece = lax.all_gather(keys, "patch", axis=1, tiled=True)
+    key_piece = jnp.concatenate(
+        lax.all_to_all(jnp.stack([keys] * lax.axis_size("patch")), "patch", 0, 0), axis=1
+    )
     value_piece = lax.all_gather(values, "patch", axis=1, tiled=True)
     count = key_piece.shape[1]
     block_len = 512

time: 492 us -> 528 us (1.073)
  local copies, waits for them, and re-layouts: 45.7 us -> 63.6 us
  matrix products: 76 us -> 90.4 us
  starting transfers between devices: 0.2 us -> 9.26 us
  waiting for transfers between devices: 311 us -> 304 us
    all_to_all x0 -> x1, waiting for transfers between devices: none -> 161 us  [body(): lax.all_to_all(jnp.stack([keys] * lax.axis_size('patch')), 'patch', 0, 0)]
    all_gather x1 -> x0, waiting for transfers between devices: 103 us -> none  [body(): key_piece = lax.all_gather(keys, 'patch', axis=1, tiled=True)]
    all_gather x1, waiting for transfers between devices: 105 us -> 31.3 us  [body(): value_piece = lax.all_gather(values, 'patch', axis=1, tiled=True)]
    dynamic_slice x0 -> x32, local copies, waits for them, and re-layouts: none -> 19.7 us  [one_block(): key_block = lax.dynamic_slice_in_dim(key_piece, offset, block_len, 1)]
    dot_general x16, matrix products: 13 us -> 29.1 us  [absorb(): jnp.einsum('vqhd,vkhd->vhqk', queries, key_heads, preferred_element_type=...]
    dynamic_slice x16, local copies, waits for them, and re-layouts: 30.6 us -> 16.5 us  [one_block(): value_block = lax.dynamic_slice_in_dim(value_piece, offset, block_len, 1)]
    all_to_all x0 -> x1, starting transfers between devices: none -> 9.1 us  [body(): lax.all_to_all(jnp.stack([keys] * lax.axis_size('patch')), 'patch', 0, 0)]
    all_to_all x0 -> x1, local copies, waits for them, and re-layouts: none -> 8.67 us  [body(): lax.all_to_all(jnp.stack([keys] * lax.axis_size('patch')), 'patch', 0, 0)]
  transfers between devices with their start and end apart: 6 -> 6, of which waited for: 5 -> 5; matrix products, arithmetic and copies ran while one was open for 28% -> 32% of each run, Pallas kernels for 0% -> 0%
where the time goes in v1:
time: 528 us; the launch traced here: 525 us
  waiting for transfers between devices  304 us (58%)
  matrix products  90.4 us (17%)
  local copies, waits for them, and re-layouts  63.6 us (12%)
  other arithmetic  42.9 us (8%)
  between operations  13.2 us (2%)
  starting transfers between devices  9.26 us (2%)
    all_to_all x1, waiting for transfers between devices, body(): lax.all_to_all(jnp.stack([keys] * lax.axis_size('patch')), 'patch', 0, 0)  161 us
    dot_general x16, matrix products, absorb(): jnp.einsum('vhqk,vkhd->vhqd', probs.astype(jnp.bfloat16), value_heads, pr...  53.1 us
    all_gather x1, waiting for transfers between devices, body(): piece = lax.all_gather(w_qkv, 'wrow', axis=0, tiled=True)  45.2 us
    reduce_scatter x1, waiting for transfers between devices, body(): lax.psum_scatter(partial_out.astype(jnp.bfloat16), 'wcol', scatter_dimens...  35.5 us
    all_gather x1, waiting for transfers between devices, body(): value_piece = lax.all_gather(values, 'patch', axis=1, tiled=True)  31.3 us
    all_gather x1, waiting for transfers between devices, body(): tile_rows = lax.all_gather(normed, 'wcol', axis=1, tiled=True)  29.8 us
    dot_general x16, matrix products, absorb(): jnp.einsum('vqhd,vkhd->vhqk', queries, key_heads, preferred_element_type=...  29.1 us
    dynamic_slice x32, local copies, waits for them, and re-layouts, one_block(): key_block = lax.dynamic_slice_in_dim(key_piece, offset, block_len, 1)  19.7 us
  transfers between devices with their start and end apart: 6, of which 5 were waited for; matrix products, arithmetic and copies ran while one was open for 32% of the time, Pallas kernels for 0%

profile of v1, /device:TPU:2, one launch (start us, length us, event | category | flops | bytes accessed | tf_op | source)
XLA Modules:
  0.0 524.5 jit_solution(7805221286097041953)
XLA Ops:
  14.8 29.8 %all-gather.6.cloned.1.call-done = bf16[1,512,1536]{2,1,0:T(8,128)(2,1)} async-done(((bf16[1,128,1536]{2,1,0:T(8,128)(2,1)}), bf16[1,512,1536]{2,1,0:T(8,128)(2,1)}) %all-gather.6.cloned.1.call-update) | async-done | bytes 1572880 | tf_op jit(solution)/shard_map/all_gather | solution.py:54
  44.6 45.2 %all-gather.8.cloned.1.call-done = bf16[1536,3,384]{0,2,1:T(8,128)(2,1)} async-done(((bf16[384,3,384]{0,2,1:T(8,128)(2,1)}), bf16[1536,3,384]{0,2,1:T(8,128)(2,1)}) %all-gather.8.cloned.1.call-update) | async-done | bytes 3538960 | tf_op jit(solution)/shard_map/all_gather | solution.py:58
  89.8 4.7 convolution_convert_fusion
  99.3 9.1 %all-to-all-start = ((bf16[16,1,512,384]{2,3,1,0:T(8,128)(2,1)}), bf16[16,1,512,384]{2,3,1,0:T(8,128)(2,1)}, u32[]{:S(2)}, u32[]{:S(2)}) async-start(bf16[16,1,512,384]{2,3,1,0:T(8,128)(2,1)} %stack.3), calls=%async_computation | async-start | bytes 12582912 | tf_op jit(solution)/shard_map/all_to_all | solution.py:72
  109.9 161.3 %all-to-all-done = bf16[16,1,512,384]{2,3,1,0:T(8,128)(2,1)} async-done(((bf16[16,1,512,384]{2,3,1,0:T(8,128)(2,1)}), bf16[16,1,512,384]{2,3,1,0:T(8,128)(2,1)}, u32[]{:S(2)}, u32[]{:S(2)}) %all-to-all-start) | async-done | bytes 6291488 | tf_op jit(solution)/shard_map/all_to_all | solution.py:72
  271.2 8.7 %copy.33 = bf16[16,1,512,384]{3,2,0,1:T(8,128)(2,1)} copy(bf16[16,1,512,384]{2,3,1,0:T(8,128)(2,1)} %all-to-all-done) | data formatting | bytes 12582912 | tf_op jit(solution)/shard_map/all_to_all | solution.py:72
  279.9 31.3 %all-gather.12.cloned.1.call-done = bf16[1,8192,1,384]{1,3,2,0:T(8,128)(2,1)} async-done(((bf16[1,512,1,384]{1,3,2,0:T(8,128)(2,1)}), bf16[1,8192,1,384]{1,3,2,0:T(8,128)(2,1)}) %all-gather.12.cloned.1.call-update) | async-done | bytes 6291472 | tf_op jit(solution)/shard_map/all_gather | solution.py:74
  311.2 163.7 %while.18 = (s32[]{:T(128)}, f32[1,3,512]{2,1,0:T(4,128)S(1)}, f32[1,3,512]{2,1,0:T(4,128)}, f32[1,3,512,128]{3,2,1,0:T(8,128)}, s32[1]{0:T(128)}, /*index=5*/bf...) while((s32[]{:T(128)}, f32[1,3,512]{2,1,0:T(4,128)S(1)}, ...), condition=%wide.region_5.6_spmd.clone, body=%wide.region_2.5_spmd.clone.sunk | while | flops 413477376 | bytes 14717259 | solution.py:84
  326.4 3.3 fusion.46
  336.7 3.4 fusion.46
  347.0 3.3 fusion.46
  357.2 3.3 fusion.46
  367.5 3.3 fusion.46
  377.7 3.3 fusion.46
  388.0 3.3 fusion.46
  398.2 3.3 fusion.46
  408.5 3.3 fusion.46
  418.8 3.3 fusion.46
  429.0 3.3 fusion.46
  439.3 3.3 fusion.46
  449.5 3.3 fusion.46
  470.0 3.3 fusion.46
  477.2 3.4 fusion.17
  480.7 35.5 %reduce-scatter.2.cloned.1.call-done = bf16[1,128,1536]{2,1,0:T(8,128)(2,1)} async-done(((bf16[1,512,1536]{2,1,0:T(8,128)(2,1)}), bf16[1,128,1536]{2,1,0:T(8,128)(2,1)}) %reduce-scatter.2.cloned.1.call-update) | async-done | bytes 393232 | tf_op jit(solution)/shard_map/reduce_scatter | solution.py:95
  (338 shorter events, 133.9 us)
Async XLA Ops:
  6.5 38.1 %all-gather.6.cloned.1.call-start = ((), (), s32[]{:S(2)}) async-start(), calls=%async_computation.2 | async-start | bytes 1966080 | tf_op jit(solution)/shard_map/all_gather | solution.py:54
  12.4 77.4 %all-gather.8.cloned.1.call-start = ((), (), s32[]{:S(2)}) async-start(), calls=%async_computation.3 | async-start | bytes 4423680 | tf_op jit(solution)/shard_map/all_gather | solution.py:58
  14.7 296.4 %all-gather.12.cloned.1.call-start = ((), (), s32[]{:S(2)}) async-start(), calls=%async_computation.6 | async-start | bytes 6684672 | tf_op jit(solution)/shard_map/all_gather | solution.py:74
  99.3 171.9 %all-to-all-start = ((bf16[16,1,512,384]{2,3,1,0:T(8,128)(2,1)}), bf16[16,1,512,384]{2,3,1,0:T(8,128)(2,1)}, u32[]{:S(2)}, u32[]{:S(2)}) async-start(bf16[16,1,512,384]{2,3,1,0:T(8,128)(2,1)} %stack.3), calls=%async_computation | async-start | bytes 12582912 | tf_op jit(solution)/shard_map/all_to_all | solution.py:72
  108.4 368.8 %all-gather.10.cloned.1.call-start = ((), (), s32[]{:S(2)}) async-start(), calls=%async_computation.4 | async-start | bytes 1474560 | tf_op jit(solution)/shard_map/all_gather | solution.py:91
  108.9 407.2 %reduce-scatter.2.cloned.1.call-start = ((), (), s32[]{:S(2)}) async-start(), calls=%async_computation.5 | async-start | bytes 1966080 | tf_op jit(solution)/shard_map/reduce_scatter | solution.py:95
  326.4 3.4 copy-start.3
  336.7 3.4 copy-start.3
  336.7 3.4 copy-start.5
  346.9 3.4 copy-start.3
  357.2 3.4 copy-start.3
  367.4 3.4 copy-start.3
  377.7 3.4 copy-start.3
  388.0 3.4 copy-start.3
  398.2 3.4 copy-start.3
  408.5 3.4 copy-start.3
  418.7 3.4 copy-start.3
  429.0 3.4 copy-start.3
  439.2 3.4 copy-start.3
  449.5 3.4 copy-start.3
  459.8 3.4 copy-start.3
  470.0 3.4 copy-start.3
  476.3 39.8 %copy-start = (bf16[1,128,1536]{2,1,0:T(8,128)(2,1)S(1)}, bf16[1,128,1536]{2,1,0:T(8,128)(2,1)}, u32[]{:S(2)}) copy-start(bf16[1,128,1536]{2,1,0:T(8,128)(2,1)} %param.7) | copy-start | bytes 1179652
  476.3 39.8 %copy-start.6 = (f32[1536]{0:T(1024)S(1)}, f32[1536]{0:T(1024)}, u32[]{:S(2)}) copy-start(f32[1536]{0:T(1024)} %get-tuple-element.198) | copy-start | bytes 18436
  (64 other events, 106.0 us)
Sparse Core Ops, SparseCore 0:
  12.5 32.0 all-gather.5
  46.4 43.3 all-gather.7
  96.1 214.9 all-gather.11
  312.9 31.2 all-gather.9
  480.8 35.3 reduce-scatter.1
